TPU v7x, 128 devices: a whole 4x4x4 slice. The times are simulated.
128 devices in a mesh: visit: 32 (over x, y, z_lo), tx: 2 (over core), ty: 2 (over z_hi).
Axes of the slice: x: 4, y: 4, z: 4 (z_hi: 2, z_lo: 2; z = z_hi * 2 + z_lo), core: 2. Of those that a mesh axis runs over, the one named last changes fastest.
Arguments:
- images: bfloat16 [32, 16, 128, 768], P('visit', None, 'ty', 'tx'), may hold values from -8 to 8
- partners: int32 [32, 16, 2], replicated, may hold values from 0 to 31, all different within a row; in each aligned block of 16 rows (0 to 15, 16 to 31, ..., all dimensions but the last counted through in order) at most 2 rows name the same one
- coverage: int32 [32, 16, 2, 16, 96], P('visit', None, None, 'ty', 'tx'), may hold values from 0 to 1, as said below
- x_filters: bfloat16 [40, 21], replicated, may hold values from -0.359375 to 0.359375
- row_filters: bfloat16 [40, 21], replicated, may hold values from -0.359375 to 0.359375
Outputs:
- coefficients: float32 [32, 16, 2, 40], P('visit', ('tx', 'ty'))
Inputs may be any that keep to these rules, and one draw needn't show every extreme that they name: In the 16 rows of one visit no visit is named more than 2 times, and in some visit's rows one visit is named exactly 2 times; the two partners of a tile differ. `coverage`: each mask is 1 on one rectangle of blocks that holds the tile's last block row and last block column, and 0 elsewhere.
All inputs are finite; a program needn't handle non-finite values.
Results may differ from a plain program's by a relative error of at most 0.00065.
Values may be sent and summed in bfloat16 or wider, within the bound.
A program may use at most 64 MiB of HBM per device.

v0:
```python
import jax
import jax.numpy as jnp
from jax import lax
from jax.sharding import PartitionSpec as P

CAP = 2
RIDGE_TERM = 0.002


def with_halo(x, sides, width):
    for axis, dim in sides:
        size, length = (lax.axis_size(axis), x.shape[dim])
        up = [(i, (i + 1) % size) for i in range(size - 1)]
        down = [(j, i) for i, j in up]
        last = lax.slice_in_dim(x, length - width, length, axis=dim)
        leading = lax.slice_in_dim(x, 0, width, axis=dim)
        before = lax.ppermute(last, axis, up)
        after = lax.ppermute(leading, axis, down)
        x = jnp.concatenate([before, x, after], axis=dim)
    return x


def horizontal_table(x_filters, block_cols, half_width):
    span_width = block_cols + 2 * half_width
    offsets = jnp.arange(span_width)[None, :] - jnp.arange(block_cols)[:, None]
    select_partner = (offsets[None, :, :] == jnp.arange(x_filters.shape[1])[:, None, None]).astype(
        jnp.float32
    )
    return jnp.einsum("kb,bcs->kcs", x_filters.astype(jnp.float32), select_partner).astype(
        jnp.bfloat16
    )


def vertical_table(row_filters, row_count, half_width):
    span_width = row_count + 2 * half_width
    offsets = jnp.arange(span_width)[:, None] - jnp.arange(row_count)[None, :]
    select_partner = (
        offsets[None, :, :] == jnp.arange(row_filters.shape[1])[:, None, None]
    ).astype(jnp.float32)
    return jnp.einsum("kb,bra->kra", row_filters.astype(jnp.float32), select_partner).astype(
        jnp.bfloat16
    )


def outgoing_choice(requests, sender_visit, capacity):
    is_sender = (requests == sender_visit).astype(jnp.int32)
    before = jnp.cumsum(is_sender, axis=1) - is_sender
    slot_ids = jnp.arange(capacity)
    picked = (is_sender[:, None, :] == 1) & (before[:, None, :] == slot_ids[None, :, None])
    return picked.astype(jnp.bfloat16)


def pack_payload(chosen_partner, message_payload):
    return jnp.einsum(
        "ekx,xo->eko", chosen_partner, message_payload, preferred_element_type=jnp.float32
    ).astype(jnp.bfloat16)


def unpack_arrivals(sources, arrived, capacity):
    count = sources.shape[0]
    same_source = sources[:, None] == sources[None, :]
    earlier = jnp.arange(count)[None, :] < jnp.arange(count)[:, None]
    slot_rank = jnp.sum(same_source & earlier, axis=1)
    position = sources * capacity + slot_rank
    total_slots = arrived.shape[0] * arrived.shape[1]
    onehot = (position[:, None] == jnp.arange(total_slots)[None, :]).astype(jnp.bfloat16)
    return jnp.dot(
        onehot, arrived.reshape(total_slots, -1), preferred_element_type=jnp.float32
    ).astype(jnp.bfloat16)


def tile_normals(tile_items, x_table, y_table, half_width, block_cols):
    extended_tile, science, blocks = tile_items
    kernel_total = y_table.shape[0]
    row_count, col_count = science.shape
    block_size = row_count // blocks.shape[1]
    weight_full = jnp.broadcast_to(
        blocks[:, :, None, :, None], (2, blocks.shape[1], block_size, blocks.shape[2], block_size)
    )
    weight_cols = jnp.transpose(weight_full.reshape(2, row_count, col_count), (0, 2, 1)).astype(
        jnp.bfloat16
    )
    science_cols = jnp.transpose(science, (1, 0))
    tile_cols = jnp.transpose(extended_tile, (0, 2, 1))
    results = []
    for partner_slot in range(2):
        total = jnp.zeros((kernel_total + 1, kernel_total + 1), jnp.float32)
        for column_block in range(col_count // block_cols):
            start = column_block * block_cols
            window = tile_cols[partner_slot, start : start + block_cols + 2 * half_width, :]
            smooth = jnp.einsum(
                "kcs,sr->kcr", x_table, window, preferred_element_type=jnp.float32
            ).astype(jnp.bfloat16)
            basis_images = jnp.einsum(
                "kcr,kra->kca", smooth, y_table, preferred_element_type=jnp.float32
            ).astype(jnp.bfloat16)
            science_part = science_cols[start : start + block_cols][None]
            stacked = jnp.concatenate([basis_images, science_part], axis=0).reshape(
                kernel_total + 1, block_cols * row_count
            )
            weights = weight_cols[partner_slot, start : start + block_cols].reshape(
                1, block_cols * row_count
            )
            total = total + jnp.einsum(
                "ip,lp->il", stacked * weights, stacked, preferred_element_type=jnp.float32
            )
        results.append(total)
    return jnp.stack(results, axis=0)


def solve_systems(sums, pixel_values):
    kernel_total = sums.shape[-1] - 1
    matrix = sums[..., :kernel_total, :kernel_total] / pixel_values + RIDGE_TERM * jnp.eye(
        kernel_total, dtype=sums.dtype
    )
    right_side = sums[..., :kernel_total, kernel_total] / pixel_values
    factor = jnp.linalg.cholesky(matrix)
    return jax.scipy.linalg.cho_solve((factor, True), right_side[..., None])[..., 0]


def body(images, partners, coverage, x_filters, row_filters):
    sender_visit = lax.axis_index("visit")
    own_tiles = images[0]
    tile_count, row_count, col_count = own_tiles.shape
    half_width = (x_filters.shape[1] - 1) // 2
    block_cols = min(col_count, 128)
    payload_shape = own_tiles.shape[1:]
    flat_payload = own_tiles.reshape(tile_count, -1)
    visit_count = partners.shape[0]
    own_partners = lax.dynamic_index_in_dim(partners, sender_visit, 0, keepdims=False)
    chosen_partner = outgoing_choice(
        partners.reshape(visit_count, 2 * tile_count), sender_visit, CAP
    )
    chosen_partner = chosen_partner.reshape(visit_count, CAP, tile_count, 2).sum(axis=3)
    arrived = lax.all_to_all(
        pack_payload(chosen_partner, flat_payload), "visit", split_axis=0, concat_axis=0, tiled=True
    )
    templates = unpack_arrivals(own_partners.reshape(2 * tile_count), arrived, CAP)
    templates = templates.reshape((2 * tile_count,) + payload_shape)
    extended_tile = with_halo(templates, (("tx", 2), ("ty", 1)), half_width)
    extended_tile = extended_tile.reshape((tile_count, 2) + extended_tile.shape[1:])
    x_table = horizontal_table(x_filters, block_cols, half_width)
    y_table = vertical_table(row_filters, row_count, half_width)
    grams = lax.map(
        lambda tile_items: tile_normals(tile_items, x_table, y_table, half_width, block_cols),
        (extended_tile, own_tiles, coverage[0]),
    )
    share_count = lax.axis_size("tx") * lax.axis_size("ty")
    totals = lax.psum(grams, ("tx", "ty"))
    share_rows = tile_count // share_count
    own_sums = lax.dynamic_slice_in_dim(
        totals, lax.axis_index(("tx", "ty")) * share_rows, share_rows, 0
    )
    pixel_values = row_count * lax.axis_size("ty") * col_count * lax.axis_size("tx")
    coefficients = solve_systems(own_sums, pixel_values)
    return coefficients[None]


def solution(mesh):
    return jax.shard_map(
        body,
        mesh=mesh,
        in_specs=(P("visit", None, "ty", "tx"), P(), P("visit", None, None, "ty", "tx"), P(), P()),
        out_specs=P("visit", ("tx", "ty"), None, None),
        check_vma=False,
    )
```

profile of v0, /device:TPU:1, one launch (start us, length us, event | category | flops | bytes accessed | tf_op | source)
XLA Modules:
  0.0 1260.5 jit_solution(8680643839919684808)
XLA Ops:
  10.2 5.0 copy.103
  15.1 9.5 all-to-all-start
  27.2 36.9 %all-to-all-done = bf16[32,2,24576]{2,1,0:T(2,128)(2,1)} async-done(((bf16[32,2,24576]{2,1,0:T(2,128)(2,1)}), bf16[32,2,24576]{2,1,0:T(2,128)(2,1)}, u32[]{:S(2)}, u32[]{:S(2)}) %all-to-all-start) | async-done | bytes 3145760 | tf_op jit(solution)/shard_map/all_to_all | solution.py:135
  64.1 4.8 reshape.148
  72.9 4.6 collective-permute-start.1
  85.4 7.1 collective-permute-start.2
  93.8 6.4 collective-permute-done.3
  101.9 5.4 pad_maximum_fusion
  107.3 4.9 copy.104
  112.2 1029.0 %while.10 = (s32[]{:T(128)}, f32[16,2,41,41]{2,3,1,0:T(8,128)}, bf16[16,2,84,404]{2,3,1,0:T(8,128)(2,1)}, bf16[40,128,148]{1,2,0:T(8,128)(2,1)S(1)}, bf16[40,84,...) while((s32[]{:T(128)}, f32[16,2,41,41]{2,3,1,0:T(8,128)}, ...), condition=%wide.region_4.5_spmd, body=%wide.region_3.4_spmd.sunk | while | flops 1265945088 | bytes 57485000 | solution.py:144
  131.6 2.9 convert_element_type.212
  167.2 2.5 constant_dynamic-update-slice_fusion.24
  195.9 2.9 convert_element_type.212
  231.5 2.5 constant_dynamic-update-slice_fusion.24
  260.2 2.9 convert_element_type.212
  324.5 2.9 convert_element_type.212
  388.8 2.9 convert_element_type.212
  424.5 2.5 constant_dynamic-update-slice_fusion.24
  453.1 2.9 convert_element_type.212
  517.4 2.9 convert_element_type.212
  581.7 2.9 convert_element_type.212
  646.1 2.9 convert_element_type.212
  710.4 2.9 convert_element_type.212
  774.6 2.9 convert_element_type.212
  839.0 2.9 convert_element_type.212
  903.3 2.9 convert_element_type.212
  967.6 2.9 convert_element_type.212
  1031.9 2.9 convert_element_type.212
  1096.2 2.9 convert_element_type.212
  1141.3 54.1 %all-reduce.2.cloned.1.call-done = f32[16,2,41,41]{2,3,1,0:T(8,128)} async-done(((f32[16,2,41,41]{2,3,1,0:T(8,128)}), f32[16,2,41,41]{2,3,1,0:T(8,128)}) %all-reduce.2.cloned.1.call-update) | async-done | bytes 215184 | tf_op jit(solution)/shard_map/psum | solution.py:149
  1197.4 29.3 %custom-call.11 = f32[4,2,40,40]{3,2,1,0:T(8,128)S(1)} custom-call(f32[4,2,40,40]{3,2,1,0:T(8,128)S(1)} %fusion.53), custom_call_target="Cholesky" | custom-call | tf_op jit(solution)/shard_map/jit(cholesky)/cholesky | solution.py:117
  1227.0 24.6 %custom-call.12 = f32[4,2,1,40,40]{3,4,2,1,0:T(8,128)S(1)} custom-call(f32[4,2,1,40,40]{4,3,2,1,0:T(8,128)S(1)} %select_bitcast_fusion), custom_call_target="InvertDiagBlocksLowerTriangular" | custom-call | tf_op jit(solution)/shard_map/jit(_cho_solve)/vmap(vmap())/triangular_solve | solution.py:118
  (1338 shorter events, 996.0 us)
Async XLA Ops:
  6.5 18.9 %copy-start = (bf16[40,21]{0,1:T(8,128)(2,1)S(1)}, bf16[40,21]{0,1:T(8,128)(2,1)}, u32[]{:S(2)}) copy-start(bf16[40,21]{0,1:T(8,128)(2,1)} %param.10) | copy-start | bytes 5044
  15.1 9.5 copy-start.17
  15.1 48.9 %all-to-all-start = ((bf16[32,2,24576]{2,1,0:T(2,128)(2,1)}), bf16[32,2,24576]{2,1,0:T(2,128)(2,1)}, u32[]{:S(2)}, u32[]{:S(2)}) async-start(bf16[32,2,24576]{2,1,0:T(2,128)(2,1)} %copy.103), calls=%async_computation | async-start | bytes 6291456 | tf_op jit(solution)/shard_map/all_to_all | solution.py:135
  24.6 1170.7 %all-reduce.2.cloned.1.call-start = ((), (), s32[]{:S(2)}) async-start(), calls=%async_computation.1 | async-start | bytes 1572864 | tf_op jit(solution)/shard_map/psum | solution.py:149
  71.6 8.7 copy-start.2
  71.7 7.1 copy-start.10
  72.9 9.2 collective-permute-start.1
  77.5 4.7 collective-permute-start
  82.1 10.4 copy-start.18
  84.0 17.9 %copy-start.12 = (bf16[32,64,10]{2,1,0:T(8,128)(2,1)S(1)}, bf16[32,64,10]{2,1,0:T(8,128)(2,1)}, u32[]{:S(2)}) copy-start(bf16[32,64,10]{2,1,0:T(8,128)(2,1)} %copy-done.11) | copy-start | bytes 122884
  84.0 16.2 %collective-permute-start.3 = (bf16[32,10,404]{2,1,0:T(8,128)(2,1)}, bf16[32,10,404]{2,1,0:T(8,128)(2,1)}, u32[]{:S(2)}, u32[]{:S(2)}) collective-permute-start(bf16[32,10,404]{2,1,0:T(8,128)(2,1)} %get-tuple-element.116), channel_id=1, source_target_pairs={{1,0},{3,2},{5,4},{7,6},{9,8},{11,10},{13,12},{15,14},{17,16},{19,... | collective-permute-start | bytes 775688 | tf_op jit(solution)/shard_map/ppermute | solution.py:18
  85.4 16.4 %collective-permute-start.2 = (bf16[32,10,404]{2,1,0:T(8,128)(2,1)}, bf16[32,10,404]{2,1,0:T(8,128)(2,1)}, u32[]{:S(2)}, u32[]{:S(2)}) collective-permute-start(bf16[32,10,404]{2,1,0:T(8,128)(2,1)} %get-tuple-element.115), channel_id=1, source_target_pairs={{0,1},{2,3},{4,5},{6,7},{8,9},{10,11},{12,13},{14,15},{16,17},{18,... | collective-permute-start | bytes 775688 | tf_op jit(solution)/shard_map/ppermute | solution.py:17
  129.4 5.1 copy-start.4
  167.2 3.6 copy-start.20
  193.7 5.1 copy-start.4
  231.5 3.6 copy-start.20
  258.0 5.1 copy-start.4
  295.8 3.6 copy-start.20
  322.3 5.1 copy-start.4
  386.6 5.1 copy-start.4
  450.9 5.1 copy-start.4
  515.3 5.1 copy-start.4
  579.6 5.1 copy-start.4
  643.9 5.1 copy-start.4
  708.2 5.1 copy-start.4
  772.5 5.1 copy-start.4
  836.8 5.1 copy-start.4
  874.6 3.6 copy-start.20
  901.1 5.1 copy-start.4
  965.4 5.1 copy-start.4
  1029.7 5.1 copy-start.4
  1094.0 5.1 copy-start.4
  (190 other events, 507.8 us)
Sparse Core Ops, SparseCore 0:
  1141.4 53.9 all-reduce.1
where the time goes:
time: 1270 us; the launch traced here: 1260 us
  local copies, waits for them, and re-layouts  676 us (53%)
  matrix products  367 us (29%)
  waiting for transfers between devices  99 us (8%)
  other arithmetic  75.9 us (6%)
  starting transfers between devices  23.9 us (2%)
  between operations  13.7 us (1%)
    concatenate x192, local copies, waits for them, and re-layouts, tile_normals(): jnp.concatenate([basis_images, science_part], axis=0)  218 us
    dot_general x96, matrix products, tile_normals(): jnp.einsum('kcr,kra->kca', smooth, y_table, preferred_element_type=jnp.fl...  213 us
    convert_element_type x96, local copies, waits for them, and re-layouts, tile_normals(): basis_images = jnp.einsum('kcr,kra->kca', smooth, y_table, preferred_elem...  159 us
    dot_general x96, matrix products, tile_normals(): jnp.einsum('ip,lp->il', stacked * weights, stacked, preferred_element_typ...  146 us
    while x464, local copies, waits for them, and re-layouts  126 us
    psum x1, waiting for transfers between devices, body(): totals = lax.psum(grams, ('tx', 'ty'))  54.1 us
    convert_element_type x16, local copies, waits for them, and re-layouts, tile_normals(): jnp.transpose(weight_full.reshape(2, row_count, col_count), (0, 2, 1))  46.4 us
    all_to_all x1, waiting for transfers between devices, body(): lax.all_to_all(pack_payload(chosen_partner, flat_payload), 'visit', split...  36.9 us
  transfers between devices with their start and end apart: 6, of which 4 were waited for; matrix products, arithmetic and copies ran while one was open for 1% of the time, Pallas kernels for 0%

commit v1 on v0

--- a/solution.py
+++ b/solution.py
@@ -146,7 +146,7 @@
         (extended_tile, own_tiles, coverage[0]),
     )
     share_count = lax.axis_size("tx") * lax.axis_size("ty")
-    totals = lax.psum(grams, ("tx", "ty"))
+    totals = jnp.sum(lax.all_gather(grams, ("tx", "ty")), axis=0)
     share_rows = tile_count // share_count
     own_sums = lax.dynamic_slice_in_dim(
         totals, lax.axis_index(("tx", "ty")) * share_rows, share_rows, 0

time: 1270 us -> 1260 us (level)
  waiting for transfers between devices: 99 us -> 43.7 us
  blocking collectives: 0 us -> 54 us
  between operations: 13.7 us -> 0.29 us
    psum x1 -> x0, waiting for transfers between devices: 54.1 us -> none  [body(): totals = lax.psum(grams, ('tx', 'ty'))]
    all_gather x0 -> x1, blocking collectives: none -> 54 us  [body(): totals = jnp.sum(lax.all_gather(grams, ('tx', 'ty')), axis=0)]
  transfers between devices with their start and end apart: 6 -> 5, of which waited for: 4 -> 4; matrix products, arithmetic and copies ran while one was open for 1% -> 1% of each run, Pallas kernels for 0% -> 0%
where the time goes in v1:
time: 1260 us; the launch traced here: 1240 us
  local copies, waits for them, and re-layouts  673 us (53%)
  matrix products  365 us (29%)
  other arithmetic  78 us (6%)
  blocking collectives  54 us (4%)
  waiting for transfers between devices  43.7 us (3%)
  starting transfers between devices  23.7 us (2%)
    concatenate x192, local copies, waits for them, and re-layouts, tile_normals(): jnp.concatenate([basis_images, science_part], axis=0)  218 us
    dot_general x96, matrix products, tile_normals(): jnp.einsum('kcr,kra->kca', smooth, y_table, preferred_element_type=jnp.fl...  213 us
    convert_element_type x96, local copies, waits for them, and re-layouts, tile_normals(): basis_images = jnp.einsum('kcr,kra->kca', smooth, y_table, preferred_elem...  159 us
    dot_general x96, matrix products, tile_normals(): jnp.einsum('ip,lp->il', stacked * weights, stacked, preferred_element_typ...  144 us
    while x464, local copies, waits for them, and re-layouts  125 us
    all_gather x1, blocking collectives, body(): totals = jnp.sum(lax.all_gather(grams, ('tx', 'ty')), axis=0)  54 us
    convert_element_type x16, local copies, waits for them, and re-layouts, tile_normals(): jnp.transpose(weight_full.reshape(2, row_count, col_count), (0, 2, 1))  46.4 us
    all_to_all x1, waiting for transfers between devices, body(): lax.all_to_all(pack_payload(chosen_partner, flat_payload), 'visit', split...  36.9 us
  transfers between devices with their start and end apart: 5, of which 4 were waited for; matrix products, arithmetic and copies ran while one was open for 1% of the time, Pallas kernels for 0%

profile of v1, /device:TPU:1, one launch (start us, length us, event | category | flops | bytes accessed | tf_op | source)
XLA Modules:
  0.0 1241.6 jit_solution(15822257855026815401)
XLA Ops:
  3.7 4.9 copy.105
  8.6 9.5 all-to-all-start
  20.6 36.9 %all-to-all-done = bf16[32,2,24576]{2,1,0:T(2,128)(2,1)} async-done(((bf16[32,2,24576]{2,1,0:T(2,128)(2,1)}), bf16[32,2,24576]{2,1,0:T(2,128)(2,1)}, u32[]{:S(2)}, u32[]{:S(2)}) %all-to-all-start) | async-done | bytes 3145760 | tf_op jit(solution)/shard_map/all_to_all | solution.py:135
  57.5 4.7 reshape.148
  65.3 4.6 collective-permute-start.1
  76.8 7.1 collective-permute-start.2
  88.6 3.9 collective-permute-done.3
  94.2 5.5 pad_maximum_fusion
  99.7 4.9 copy.106
  104.6 1023.4 %while.10 = (s32[]{:T(128)}, f32[16,2,41,41]{3,1,2,0:T(2,128)}, bf16[16,2,84,404]{2,3,1,0:T(8,128)(2,1)}, bf16[40,128,148]{1,2,0:T(8,128)(2,1)S(1)}, bf16[40,84,...) while((s32[]{:T(128)}, f32[16,2,41,41]{3,1,2,0:T(2,128)}, ...), condition=%wide.region_4.5_spmd, body=%wide.region_3.4_spmd.sunk | while | flops 1265945088 | bytes 57450936 | solution.py:144
  123.9 2.9 convert_element_type.212
  187.9 2.9 convert_element_type.212
  251.8 2.9 convert_element_type.212
  315.8 2.9 convert_element_type.212
  351.3 2.5 constant_dynamic-update-slice_fusion.22
  379.8 2.9 convert_element_type.212
  443.7 2.9 convert_element_type.212
  479.2 2.5 constant_dynamic-update-slice_fusion.22
  507.7 2.9 convert_element_type.212
  571.7 2.9 convert_element_type.212
  635.6 2.9 convert_element_type.212
  699.6 2.9 convert_element_type.212
  763.6 2.9 convert_element_type.212
  827.5 2.9 convert_element_type.212
  891.5 2.9 convert_element_type.212
  955.5 2.9 convert_element_type.212
  1019.4 2.9 convert_element_type.212
  1083.4 2.9 convert_element_type.212
  1128.0 54.0 %all-gather = f32[64,2,41,41]{3,1,2,0:T(2,128)} all-gather(f32[16,2,41,41]{3,1,2,0:T(2,128)} %get-tuple-element.42), channel_id=2, replica_groups=mesh['visit'=32,'tx'=2,'ty'=2] {'tx','ty'}, dimensions={0}, use_global_device_ids=true | all-gather | bytes 1075840 | tf_op jit(solution)/shard_map/all_gather | solution.py:149
  1182.0 3.4 reduce_sum.32
  1185.7 29.3 %custom-call.11 = f32[4,2,40,40]{3,2,1,0:T(8,128)S(1)} custom-call(f32[4,2,40,40]{3,2,1,0:T(8,128)S(1)} %fusion.52), custom_call_target="Cholesky" | custom-call | tf_op jit(solution)/shard_map/jit(cholesky)/cholesky | solution.py:117
  1215.3 24.6 %custom-call.12 = f32[4,2,1,40,40]{3,4,2,1,0:T(8,128)S(1)} custom-call(f32[4,2,1,40,40]{4,3,2,1,0:T(8,128)S(1)} %select_bitcast_fusion), custom_call_target="InvertDiagBlocksLowerTriangular" | custom-call | tf_op jit(solution)/shard_map/jit(_cho_solve)/vmap(vmap())/triangular_solve | solution.py:118
  (1327 shorter events, 992.3 us)
Async XLA Ops:
  0.0 18.8 %copy-start = (bf16[40,21]{0,1:T(8,128)(2,1)S(1)}, bf16[40,21]{0,1:T(8,128)(2,1)}, u32[]{:S(2)}) copy-start(bf16[40,21]{0,1:T(8,128)(2,1)} %param.10) | copy-start | bytes 5044
  8.6 9.5 copy-start.17
  8.6 48.9 %all-to-all-start = ((bf16[32,2,24576]{2,1,0:T(2,128)(2,1)}), bf16[32,2,24576]{2,1,0:T(2,128)(2,1)}, u32[]{:S(2)}, u32[]{:S(2)}) async-start(bf16[32,2,24576]{2,1,0:T(2,128)(2,1)} %copy.105), calls=%async_computation | async-start | bytes 6291456 | tf_op jit(solution)/shard_map/all_to_all | solution.py:135
  65.0 10.4 copy-start.2
  65.1 6.2 copy-start.19
  65.3 7.2 collective-permute-start.1
  69.9 3.8 collective-permute-start
  72.5 11.4 copy-start.9
  75.5 17.1 %collective-permute-start.3 = (bf16[32,10,404]{2,1,0:T(8,128)(2,1)}, bf16[32,10,404]{2,1,0:T(8,128)(2,1)}, u32[]{:S(2)}, u32[]{:S(2)}) collective-permute-start(bf16[32,10,404]{2,1,0:T(8,128)(2,1)} %get-tuple-element.116), channel_id=1, source_target_pairs={{1,0},{3,2},{5,4},{7,6},{9,8},{11,10},{13,12},{15,14},{17,16},{19,... | collective-permute-start | bytes 775688 | tf_op jit(solution)/shard_map/ppermute | solution.py:18
  76.8 17.5 %collective-permute-start.2 = (bf16[32,10,404]{2,1,0:T(8,128)(2,1)}, bf16[32,10,404]{2,1,0:T(8,128)(2,1)}, u32[]{:S(2)}, u32[]{:S(2)}) collective-permute-start(bf16[32,10,404]{2,1,0:T(8,128)(2,1)} %get-tuple-element.115), channel_id=1, source_target_pairs={{0,1},{2,3},{4,5},{6,7},{8,9},{10,11},{12,13},{14,15},{16,17},{18,... | collective-permute-start | bytes 775688 | tf_op jit(solution)/shard_map/ppermute | solution.py:17
  121.7 5.1 copy-start.3
  159.4 3.6 copy-start.21
  185.7 5.1 copy-start.3
  249.7 5.1 copy-start.3
  313.6 5.1 copy-start.3
  377.6 5.1 copy-start.3
  441.6 5.1 copy-start.3
  479.2 3.6 copy-start.21
  505.5 5.1 copy-start.3
  543.2 3.6 copy-start.21
  569.5 5.1 copy-start.3
  633.4 5.1 copy-start.3
  671.1 3.6 copy-start.21
  697.4 5.1 copy-start.3
  761.4 5.1 copy-start.3
  799.0 3.6 copy-start.21
  825.3 5.1 copy-start.3
  889.3 5.1 copy-start.3
  953.3 5.1 copy-start.3
  1017.2 5.1 copy-start.3
  1081.2 5.1 copy-start.3
  1185.4 29.8 %copy-start.18 = (pred[40,40]{1,0:T(8,128)(4,1)S(1)}, pred[40,40]{1,0:T(8,128)(4,1)}, u32[]{:S(2)}) copy-start(pred[40,40]{1,0:T(8,128)(4,1)} %iota_compare_fusion.10) | copy-start | bytes 4804
  (190 other events, 502.4 us)
